TPU v7x, 32 devices: a whole 2x2x4 slice. The times are simulated.
32 devices in a mesh: pairs: 2 (over x), src: 8 (over z, y), tgt: 2 (over core).
Axes of the slice: x: 2, y: 2, z: 4, core: 2. Of those that a mesh axis runs over, the one named last changes fastest.
Arguments:
- src_feat: float32 [2048, 32], P(('pairs', 'src'), 'tgt'), parts along dimension 0, may hold values from -0.72 to 0.72
- tgt_feat: float32 [32768, 32], P(('pairs', 'tgt'), 'src'), parts along dimension 0, may hold values from -0.72 to 0.72
- tgt_dual: float32 [32768], P(('pairs', 'tgt')), parts along dimension 0, may hold values from -6 to 6
- core_matrix: float32 [68, 34], P('pairs'), parts along dimension 0, may hold values from -3 to 3
Outputs:
- src_dual: float32 [2048], P(('pairs', 'src')), parts along dimension 0
- tgt_dual_out: float32 [32768], P(('pairs', 'tgt')), parts along dimension 0
- core_out: float32 [68, 34], P('pairs'), parts along dimension 0
There are 2 independent parts, one for each index of `pairs`. A program takes and returns all parts, laid end to end along the dimension named above; each array names one. Nothing has to cross between parts.
All inputs are finite; a program needn't handle non-finite values.
Results may differ from a plain program's by a relative error of at most 0.0003.
Values sent between devices are 32-bit elements; how exact they have to be, the bound alone decides.
No kernel may reach another device: no remote copies, remote signals or barrier semaphores. Data moves between devices by JAX's collectives and lax.ppermute only.
A program may use at most 64 MiB of HBM per device.

v0:
```python
import jax
import jax.numpy as jnp
from jax import lax
from jax.sharding import PartitionSpec as P

OUTER = 2
EPSILON = 0.02
HIGH = lax.Precision.HIGHEST


def merged(array, axis, combine):
    everything = jax.tree.map(lambda part: lax.all_gather(part, axis), array)
    leading = jax.tree.map(lambda part: part[0], everything)

    def step(k, so_far):
        return combine(so_far, jax.tree.map(lambda part: part[k], everything))

    return lax.fori_loop(1, lax.axis_size(axis), step, leading)


def lifted(values):
    squares = jnp.sum(values * values, axis=1, keepdims=True)
    ones = jnp.ones_like(squares)
    left = jnp.concatenate([squares, ones, -2.0 * values], axis=1)
    right = jnp.concatenate([ones, squares, values], axis=1)
    return (left, right)


def merge_logsum(earlier, later):
    top = jnp.maximum(earlier[0], later[0])
    return (top, earlier[1] * jnp.exp(earlier[0] - top) + later[1] * jnp.exp(later[0] - top))


def shards(src_feat, tgt_feat, tgt_dual, core_matrix):
    src_rows = lax.all_gather(src_feat, "tgt", axis=1, tiled=True)
    tgt_rows = lax.all_gather(tgt_feat, "src", axis=1, tiled=True)
    src_left, src_right = lifted(src_rows)
    tgt_left, tgt_right = lifted(tgt_rows)
    src_count = lax.axis_size("src")
    tgt_count = lax.axis_size("tgt")
    row_count = src_rows.shape[0]
    col_count = tgt_rows.shape[0]
    log_src = -jnp.log(jnp.float32(row_count * src_count))
    log_tgt = -jnp.log(jnp.float32(col_count * tgt_count))
    src_dual = jnp.zeros((row_count,), jnp.float32)
    for outer_step in range(OUTER):
        projected = jnp.dot(src_left, core_matrix, precision=HIGH)
        linear = jnp.dot(projected, tgt_right.T, precision=HIGH)
        row_logits = (tgt_dual[None, :] - linear) / EPSILON
        row_max = jnp.max(row_logits, axis=1)
        row_total = jnp.sum(jnp.exp(row_logits - row_max[:, None]), axis=1)
        row_max, row_total = merged((row_max, row_total), "tgt", merge_logsum)
        src_dual = EPSILON * log_src - EPSILON * (row_max + jnp.log(row_total))
        col_logits = (src_dual[:, None] - linear) / EPSILON
        col_max = jnp.max(col_logits, axis=0)
        col_exp = jnp.exp(col_logits - col_max[None, :])
        col_total = jnp.sum(col_exp, axis=0)
        piece_max, piece_total = (
            lax.all_to_all(col_max[None, :], "src", split_axis=1, concat_axis=0, tiled=True),
            lax.all_to_all(col_total[None, :], "src", split_axis=1, concat_axis=0, tiled=True),
        )
        whole_max = jnp.max(piece_max, axis=0)
        whole_total = jnp.sum(piece_total * jnp.exp(piece_max - whole_max[None, :]), axis=0)
        dual_piece = EPSILON * log_tgt - EPSILON * (whole_max + jnp.log(whole_total))
        tgt_dual = lax.all_gather(dual_piece, "src", axis=0, tiled=True)
        coupling = jnp.exp((src_dual[:, None] + tgt_dual[None, :] - linear) / EPSILON)
        weighted = jnp.dot(coupling, tgt_left, precision=HIGH)
        core_part = jnp.dot(src_right.T, weighted, precision=HIGH)
        core_matrix = -2.0 * lax.psum(core_part, ("src", "tgt"))
    return (src_dual, tgt_dual, core_matrix)


def solution(mesh):
    placed = (
        P(("pairs", "src"), "tgt"),
        P(("pairs", "tgt"), "src"),
        P(("pairs", "tgt")),
        P("pairs", None),
    )
    return jax.shard_map(
        shards,
        mesh=mesh,
        in_specs=placed,
        out_specs=(P(("pairs", "src")), P(("pairs", "tgt")), P("pairs", None)),
        check_vma=False,
    )
```

profile of v0, /device:TPU:0, one launch (start us, length us, event | category | flops | bytes accessed | tf_op | source)
XLA Modules:
  0.0 312.0 jit_solution(1951934580604606527)
XLA Ops:
  7.9 2.2 all_gather.36
  10.4 42.7 %all-gather.11.cloned.1.call-done = f32[8,4,8192]{2,1,0:T(4,128)} async-done(((f32[1,4,8192]{2,1,0:T(4,128)}), f32[8,4,8192]{2,1,0:T(4,128)}) %all-gather.11.cloned.1.call-update) | async-done | bytes 1048592 | tf_op jit(solution)/shard_map/all_gather | solution.py:36
  55.0 3.8 %fusion.10 = (f32[128]{0:T(128)S(1)}, f32[128,8192]{1,0:T(8,128)S(1)}) fusion(f32[8192]{0:T(1024)S(1)} %copy-done.3, f32[128,34]{1,0:T(8,128)S(1)} %fusion.32, f32[8192,32]{0,1:T(8,128)S(1)} %bitcast.89, f32[8192,1]{0,1:T(1,128)S(1)} %bitcast.91, f32[8192,1]{0,1:T(1,128)S(1)} %broadcast_in_dim.10), kind=kOutput, calls=%fused_computation.18 | convolution fusion | flops 431521664 | bytes 5359104 | tf_op jit(solution)/shard_map/dot_general | solution.py:48
  59.8 1.8 all-gather.6
  61.6 1.8 all-gather.5
  64.5 3.3 %all-to-all-start = ((f32[1,8,1024]{2,0,1:T(1,128)}), f32[1,8,1024]{2,0,1:T(1,128)S(1)}, u32[]{:S(2)}, u32[]{:S(2)}) async-start(f32[1,8,1024]{2,0,1:T(1,128)} %bitcast.11), calls=%async_computation | async-start | bytes 65536 | tf_op jit(solution)/shard_map/all_to_all | solution.py:59
  67.9 3.7 %exponential_reduce_fusion.2 = f32[8192]{0:T(1024)} fusion(f32[128,8192]{1,0:T(8,128)} %copy-done.2, f32[8192]{0:T(1024)} %fusion.11, f32[128]{0:T(128)S(1)} %multiply_subtract_fusion.3), kind=kLoop, calls=%fused_computation.14 | loop fusion | flops 4186112 | bytes 4260352 | tf_op jit(solution)/shard_map/reduce_sum | solution.py:57
  71.6 2.9 all-to-all-done
  74.6 3.3 %all-to-all-start.1 = ((f32[1,8,1024]{2,0,1:T(1,128)}), f32[1,8,1024]{2,0,1:T(1,128)S(1)}, u32[]{:S(2)}, u32[]{:S(2)}) async-start(f32[1,8,1024]{2,0,1:T(1,128)} %bitcast.12), calls=%async_computation.1 | async-start | bytes 65536 | tf_op jit(solution)/shard_map/all_to_all | solution.py:60
  77.9 6.6 %all-to-all-done.1 = f32[1,8,1024]{2,0,1:T(1,128)S(1)} async-done(((f32[1,8,1024]{2,0,1:T(1,128)}), f32[1,8,1024]{2,0,1:T(1,128)S(1)}, u32[]{:S(2)}, u32[]{:S(2)}) %all-to-all-start.1) | async-done | bytes 32800 | tf_op jit(solution)/shard_map/all_to_all | solution.py:60
  84.6 30.6 %all_gather.42 = f32[8192]{0:T(1024)S(1)} all-gather(f32[1024]{0:T(1024)S(1)} %multiply_subtract_fusion.1), channel_id=1, replica_groups=mesh['pairs'=2,'src'=8,'tgt'=2] {'src'}, dimensions={0}, use_global_device_ids=true | all-gather | bytes 36864 | tf_op jit(solution)/shard_map/all_gather | solution.py:65
  115.2 6.2 %fusion.5 = f32[128,34]{1,0:T(8,128)S(1)} fusion(f32[128,8192]{1,0:T(8,128)} %copy-done.2, f32[8192]{0:T(1024)S(1)} %all_gather.42, f32[128]{0:T(128)S(1)} %multiply_subtract_fusion.3, f32[8192,32]{0,1:T(8,128)S(1)} %get-tuple-element.27, f32[8192,1]{0,1:T(1,128)S(1)} %broadcast_in_dim.10, f32[8192,1]{0,1:T(1,128)S(1)} %bitcast.92), kind=kOutput, calls=%fused_computation.9 | convolution fusion | flops 431521792 | bytes 5359104 | tf_op jit(solution)/shard_map/dot_general | solution.py:67
  121.6 57.8 %psum.14 = f32[34,34]{1,0:T(8,128)S(1)} all-reduce(f32[34,34]{1,0:T(8,128)S(1)} %fusion.31), channel_id=1, replica_groups=mesh['pairs'=2,'src'=8,'tgt'=2] {'src','tgt'}, use_global_device_ids=true, to_apply=%region_8.0 | all-reduce | flops 1156 | bytes 9248 | tf_op jit(solution)/shard_map/psum | solution.py:69
  179.7 3.8 %fusion.12 = (f32[128]{0:T(128)S(1)}, f32[128,8192]{1,0:T(8,128)S(1)}) fusion(f32[8192]{0:T(1024)S(1)} %all_gather.42, f32[128,34]{1,0:T(8,128)S(1)} %fusion.28, f32[8192,32]{0,1:T(8,128)S(1)} %bitcast.90, f32[8192,1]{0,1:T(1,128)S(1)} %bitcast.93, f32[8192,1]{0,1:T(1,128)S(1)} %broadcast_in_dim.10), kind=kOutput, calls=%fused_computation.20 | convolution fusion | flops 431521664 | bytes 5359104 | tf_op jit(solution)/shard_map/dot_general | solution.py:48
  184.5 1.8 all-gather.8
  186.3 1.8 all-gather.7
  189.3 3.3 %all-to-all-start.2 = ((f32[1,8,1024]{2,0,1:T(1,128)}), f32[1,8,1024]{2,0,1:T(1,128)S(1)}, u32[]{:S(2)}, u32[]{:S(2)}) async-start(f32[1,8,1024]{2,0,1:T(1,128)} %bitcast.19), calls=%async_computation.2 | async-start | bytes 65536 | tf_op jit(solution)/shard_map/all_to_all | solution.py:59
  192.6 3.7 %exponential_reduce_fusion = f32[8192]{0:T(1024)} fusion(f32[128,8192]{1,0:T(8,128)} %copy-done.1, f32[8192]{0:T(1024)} %fusion.13, f32[128]{0:T(128)S(1)} %multiply_subtract_fusion.2), kind=kLoop, calls=%fused_computation.5 | loop fusion | flops 4186112 | bytes 4260352 | tf_op jit(solution)/shard_map/reduce_sum | solution.py:57
  196.4 2.9 all-to-all-done.2
  199.3 3.3 %all-to-all-start.3 = ((f32[1,8,1024]{2,0,1:T(1,128)}), f32[1,8,1024]{2,0,1:T(1,128)S(1)}, u32[]{:S(2)}, u32[]{:S(2)}) async-start(f32[1,8,1024]{2,0,1:T(1,128)} %bitcast.20), calls=%async_computation.3 | async-start | bytes 65536 | tf_op jit(solution)/shard_map/all_to_all | solution.py:60
  202.7 6.6 %all-to-all-done.3 = f32[1,8,1024]{2,0,1:T(1,128)S(1)} async-done(((f32[1,8,1024]{2,0,1:T(1,128)}), f32[1,8,1024]{2,0,1:T(1,128)S(1)}, u32[]{:S(2)}, u32[]{:S(2)}) %all-to-all-start.3) | async-done | bytes 32800 | tf_op jit(solution)/shard_map/all_to_all | solution.py:60
  209.3 30.6 %all_gather.47 = f32[8192]{0:T(1024)S(1)} all-gather(f32[1024]{0:T(1024)S(1)} %multiply_subtract_fusion), channel_id=1, replica_groups=mesh['pairs'=2,'src'=8,'tgt'=2] {'src'}, dimensions={0}, use_global_device_ids=true | all-gather | bytes 36864 | tf_op jit(solution)/shard_map/all_gather | solution.py:65
  239.9 6.2 %fusion = f32[128,34]{1,0:T(8,128)S(1)} fusion(f32[128,8192]{1,0:T(8,128)} %copy-done.1, f32[8192]{0:T(1024)S(1)} %all_gather.47, f32[128]{0:T(128)S(1)} %multiply_subtract_fusion.2, f32[8192,32]{0,1:T(8,128)S(1)} %get-tuple-element.27, f32[8192,1]{0,1:T(1,128)S(1)} %broadcast_in_dim.10, f32[8192,1]{0,1:T(1,128)S(1)} %bitcast.94), kind=kOutput, calls=%fused_computation | convolution fusion | flops 431521792 | bytes 5359104 | tf_op jit(solution)/shard_map/dot_general | solution.py:67
  246.3 57.6 %psum.15 = f32[34,34]{1,0:T(8,128)S(1)} all-reduce(f32[34,34]{1,0:T(8,128)S(1)} %fusion.30), channel_id=1, replica_groups=mesh['pairs'=2,'src'=8,'tgt'=2] {'src','tgt'}, use_global_device_ids=true, to_apply=%region_15.0 | all-reduce | flops 1156 | bytes 9248 | tf_op jit(solution)/shard_map/psum | solution.py:69
  (35 shorter events, 9.2 us)
Async XLA Ops:
  7.2 3.0 copy-start
  7.2 47.8 %copy-start.3 = (f32[8192]{0:T(1024)S(1)}, f32[8192]{0:T(1024)}, u32[]{:S(2)}) copy-start(f32[8192]{0:T(1024)} %param.6) | copy-start | bytes 98308
  7.2 46.0 %all-gather.11.cloned.1.call-start = ((), (), s32[]{:S(2)}) async-start(), calls=%async_computation.4 | async-start | bytes 1179648 | tf_op jit(solution)/shard_map/all_gather | solution.py:36
  58.8 5.8 %copy-start.2 = (f32[128,8192]{1,0:T(8,128)}, f32[128,8192]{1,0:T(8,128)S(1)}, u32[]{:S(2)}) copy-start(f32[128,8192]{1,0:T(8,128)S(1)} %get-tuple-element.38) | copy-start | bytes 12582916
  64.5 10.0 %all-to-all-start = ((f32[1,8,1024]{2,0,1:T(1,128)}), f32[1,8,1024]{2,0,1:T(1,128)S(1)}, u32[]{:S(2)}, u32[]{:S(2)}) async-start(f32[1,8,1024]{2,0,1:T(1,128)} %bitcast.11), calls=%async_computation | async-start | bytes 65536 | tf_op jit(solution)/shard_map/all_to_all | solution.py:59
  74.6 10.0 %all-to-all-start.1 = ((f32[1,8,1024]{2,0,1:T(1,128)}), f32[1,8,1024]{2,0,1:T(1,128)S(1)}, u32[]{:S(2)}, u32[]{:S(2)}) async-start(f32[1,8,1024]{2,0,1:T(1,128)} %bitcast.12), calls=%async_computation.1 | async-start | bytes 65536 | tf_op jit(solution)/shard_map/all_to_all | solution.py:60
  183.5 5.8 %copy-start.1 = (f32[128,8192]{1,0:T(8,128)}, f32[128,8192]{1,0:T(8,128)S(1)}, u32[]{:S(2)}) copy-start(f32[128,8192]{1,0:T(8,128)S(1)} %get-tuple-element.40) | copy-start | bytes 12582916
  188.1 51.8 %copy-start.4 = (f32[128]{0:T(128)}, f32[128]{0:T(128)S(1)}, u32[]{:S(2)}) copy-start(f32[128]{0:T(128)S(1)} %multiply_subtract_fusion.2) | copy-start | bytes 1540
  189.3 10.0 %all-to-all-start.2 = ((f32[1,8,1024]{2,0,1:T(1,128)}), f32[1,8,1024]{2,0,1:T(1,128)S(1)}, u32[]{:S(2)}, u32[]{:S(2)}) async-start(f32[1,8,1024]{2,0,1:T(1,128)} %bitcast.19), calls=%async_computation.2 | async-start | bytes 65536 | tf_op jit(solution)/shard_map/all_to_all | solution.py:59
  199.3 10.0 %all-to-all-start.3 = ((f32[1,8,1024]{2,0,1:T(1,128)}), f32[1,8,1024]{2,0,1:T(1,128)S(1)}, u32[]{:S(2)}, u32[]{:S(2)}) async-start(f32[1,8,1024]{2,0,1:T(1,128)} %bitcast.20), calls=%async_computation.3 | async-start | bytes 65536 | tf_op jit(solution)/shard_map/all_to_all | solution.py:60
Sparse Core Ops, SparseCore 0:
  10.1 42.9 all-gather.10
where the time goes:
time: 313 us; the launch traced here: 312 us
  blocking collectives  186 us (59%)
  waiting for transfers between devices  62.4 us (20%)
  matrix products  21 us (7%)
  between operations  14.2 us (5%)
  starting transfers between devices  13.4 us (4%)
  other arithmetic  12.7 us (4%)
    psum x2, blocking collectives, shards(): core_matrix = -2.0 * lax.psum(core_part, ('src', 'tgt'))  115 us
    all_gather x2, blocking collectives, shards(): tgt_dual = lax.all_gather(dual_piece, 'src', axis=0, tiled=True)  61.2 us
    all_gather x1, waiting for transfers between devices, shards(): tgt_rows = lax.all_gather(tgt_feat, 'src', axis=1, tiled=True)  42.7 us
    all_to_all x2, waiting for transfers between devices, shards(): lax.all_to_all(col_total[None, :], 'src', split_axis=1, concat_axis=0, ti...  13.2 us
    dot_general x2, matrix products, shards(): weighted = jnp.dot(coupling, tgt_left, precision=HIGH)  12.4 us
    dot_general x2, matrix products, shards(): linear = jnp.dot(projected, tgt_right.T, precision=HIGH)  7.61 us
    reduce_sum x2, other arithmetic, shards(): col_total = jnp.sum(col_exp, axis=0)  7.45 us
    all_gather x4, blocking collectives, merged(): everything = jax.tree.map(lambda part: lax.all_gather(part, axis), array)  7.19 us
  transfers between devices with their start and end apart: 5, of which 5 were waited for; matrix products, arithmetic and copies ran while one was open for 3% of the time, Pallas kernels for 0%

commit v1 on v0

--- a/solution.py
+++ b/solution.py
@@ -6,6 +6,19 @@
 OUTER = 2
 EPSILON = 0.02
 HIGH = lax.Precision.HIGHEST
+
+
+def _refer_points(lane_axis, message):
+    low = lax.psum(1, lane_axis)
+    t_next = lax.axis_index(lane_axis)
+    side_arr, right_arr, formed = (low, t_next, message.shape[1])
+    left_arr, part_now = (message, 1)
+    while part_now < side_arr:
+        item_now = tuple(((idx, (idx - part_now) % side_arr) for idx in range(side_arr)))
+        response = lax.ppermute(left_arr, lane_axis, item_now)
+        left_arr = jnp.concatenate([left_arr, response], axis=1)
+        part_now = 2 * part_now
+    return jnp.roll(left_arr, right_arr * formed, axis=1)
 
 
 def merged(array, axis, combine):
@@ -33,7 +46,7 @@
 
 def shards(src_feat, tgt_feat, tgt_dual, core_matrix):
     src_rows = lax.all_gather(src_feat, "tgt", axis=1, tiled=True)
-    tgt_rows = lax.all_gather(tgt_feat, "src", axis=1, tiled=True)
+    tgt_rows = _refer_points("src", tgt_feat)
     src_left, src_right = lifted(src_rows)
     tgt_left, tgt_right = lifted(tgt_rows)
     src_count = lax.axis_size("src")

time: 313 us -> 301 us (0.962)
  between operations: 14.2 us -> 0.84 us
  waiting for transfers between devices: 62.4 us -> 49.2 us
  starting transfers between devices: 13.4 us -> 24.4 us
    all_gather x1 -> x0, waiting for transfers between devices: 42.7 us -> none  [shards(): tgt_rows = lax.all_gather(tgt_feat, 'src', axis=1, tiled=True)]
    ppermute x0 -> x3, waiting for transfers between devices: none -> 30.1 us  [_refer_points(): response = lax.ppermute(left_arr, lane_axis, item_now)]
    ppermute x0 -> x3, starting transfers between devices: none -> 8.03 us  [_refer_points(): response = lax.ppermute(left_arr, lane_axis, item_now)]
  transfers between devices with their start and end apart: 5 -> 7, of which waited for: 5 -> 7; matrix products, arithmetic and copies ran while one was open for 3% -> 3% of each run, Pallas kernels for 0% -> 0%
where the time goes in v1:
time: 301 us; the launch traced here: 300 us
  blocking collectives  186 us (62%)
  waiting for transfers between devices  49.2 us (16%)
  starting transfers between devices  24.4 us (8%)
  matrix products  21 us (7%)
  other arithmetic  15.7 us (5%)
    psum x2, blocking collectives, shards(): core_matrix = -2.0 * lax.psum(core_part, ('src', 'tgt'))  115 us
    all_gather x2, blocking collectives, shards(): tgt_dual = lax.all_gather(dual_piece, 'src', axis=0, tiled=True)  61.2 us
    ppermute x3, waiting for transfers between devices, _refer_points(): response = lax.ppermute(left_arr, lane_axis, item_now)  30.1 us
    all_to_all x2, waiting for transfers between devices, shards(): lax.all_to_all(col_total[None, :], 'src', split_axis=1, concat_axis=0, ti...  13.2 us
    dot_general x2, matrix products, shards(): weighted = jnp.dot(coupling, tgt_left, precision=HIGH)  12.4 us
    all_to_all x2, starting transfers between devices, shards(): lax.all_to_all(col_max[None, :], 'src', split_axis=1, concat_axis=0, tile...  9.7 us
    ppermute x3, starting transfers between devices, _refer_points(): response = lax.ppermute(left_arr, lane_axis, item_now)  8.03 us
    dot_general x2, matrix products, shards(): linear = jnp.dot(projected, tgt_right.T, precision=HIGH)  7.6 us
  transfers between devices with their start and end apart: 7, of which 7 were waited for; matrix products, arithmetic and copies ran while one was open for 3% of the time, Pallas kernels for 0%

profile of v1, /device:TPU:0, one launch (start us, length us, event | category | flops | bytes accessed | tf_op | source)
XLA Modules:
  0.0 300.0 jit_solution(9890548215445477040)
XLA Ops:
  0.6 6.1 %collective-permute-start = (f32[8192,4]{0,1:T(4,128)}, f32[8192,4]{0,1:T(4,128)S(1)}, u32[]{:S(2)}, u32[]{:S(2)}) collective-permute-start(f32[8192,4]{0,1:T(4,128)} %param.5), channel_id=1, source_target_pairs={{0,14},{2,0},{4,2},{6,4},{8,6},{10,8},{12,10},{14,12},{1,15},{3,1}... | collective-permute-start | bytes 393224 | tf_op jit(solution)/shard_map/ppermute | solution.py:18
  6.7 3.1 %collective-permute-done = f32[8192,4]{0,1:T(4,128)S(1)} collective-permute-done((f32[8192,4]{0,1:T(4,128)}, f32[8192,4]{0,1:T(4,128)S(1)}, u32[]{:S(2)}, u32[]{:S(2)}) %collective-permute-start) | collective-permute-done | bytes 131104 | tf_op jit(solution)/shard_map/ppermute | solution.py:18
  12.2 5.8 %collective-permute-done.1 = f32[8192,8]{0,1:T(8,128)S(1)} collective-permute-done((f32[8192,8]{0,1:T(8,128)S(1)}, f32[8192,8]{0,1:T(8,128)S(1)}, u32[]{:S(2)}, u32[]{:S(2)}) %collective-permute-start.1) | collective-permute-done | bytes 262176 | tf_op jit(solution)/shard_map/ppermute | solution.py:18
  19.5 2.0 all_gather.33
  21.8 21.3 %collective-permute-done.2 = f32[8192,16]{0,1:T(8,128)S(1)} collective-permute-done((f32[8192,16]{0,1:T(8,128)S(1)}, f32[8192,16]{0,1:T(8,128)S(1)}, u32[]{:S(2)}, u32[]{:S(2)}) %collective-permute-start.2) | collective-permute-done | bytes 524320 | tf_op jit(solution)/shard_map/ppermute | solution.py:18
  43.2 2.3 concatenate.29
  46.7 3.8 %fusion.10 = (f32[128]{0:T(128)S(1)}, f32[128,8192]{1,0:T(8,128)S(1)}) fusion(f32[8192]{0:T(1024)S(1)} %copy-done.4, f32[128,34]{1,0:T(8,128)S(1)} %fusion.32, f32[8192,32]{0,1:T(8,128)S(1)} %get-tuple-element.28, f32[8192,1]{0,1:T(1,128)S(1)} %bitcast.83, f32[8192,1]{0,1:T(1,128)S(1)} %broadcast_in_dim.10), kind=kOutput, calls=%fused_computation.18 | convolution fusion | flops 431521664 | bytes 5359104 | tf_op jit(solution)/shard_map/dot_general | solution.py:61
  56.3 6.4 %all-to-all-start = ((f32[1,8,1024]{2,0,1:T(1,128)}), f32[1,8,1024]{2,0,1:T(1,128)S(1)}, u32[]{:S(2)}, u32[]{:S(2)}) async-start(f32[1,8,1024]{2,0,1:T(1,128)} %bitcast.8), calls=%async_computation | async-start | bytes 65536 | tf_op jit(solution)/shard_map/all_to_all | solution.py:72
  62.7 3.7 %exponential_reduce_fusion.2 = f32[8192]{0:T(1024)} fusion(f32[128,8192]{1,0:T(8,128)} %copy-done.2, f32[8192]{0:T(1024)} %fusion.11, f32[128]{0:T(128)S(1)} %multiply_subtract_fusion.3), kind=kLoop, calls=%fused_computation.14 | loop fusion | flops 4186112 | bytes 4260352 | tf_op jit(solution)/shard_map/reduce_sum | solution.py:70
  66.4 3.0 all-to-all-done
  69.4 3.3 %all-to-all-start.1 = ((f32[1,8,1024]{2,0,1:T(1,128)}), f32[1,8,1024]{2,0,1:T(1,128)S(1)}, u32[]{:S(2)}, u32[]{:S(2)}) async-start(f32[1,8,1024]{2,0,1:T(1,128)} %bitcast.9), calls=%async_computation.1 | async-start | bytes 65536 | tf_op jit(solution)/shard_map/all_to_all | solution.py:73
  72.7 6.6 %all-to-all-done.1 = f32[1,8,1024]{2,0,1:T(1,128)S(1)} async-done(((f32[1,8,1024]{2,0,1:T(1,128)}), f32[1,8,1024]{2,0,1:T(1,128)S(1)}, u32[]{:S(2)}, u32[]{:S(2)}) %all-to-all-start.1) | async-done | bytes 32800 | tf_op jit(solution)/shard_map/all_to_all | solution.py:73
  79.4 30.6 %all_gather.38 = f32[8192]{0:T(1024)S(1)} all-gather(f32[1024]{0:T(1024)S(1)} %multiply_subtract_fusion.1), channel_id=1, replica_groups=mesh['pairs'=2,'src'=8,'tgt'=2] {'src'}, dimensions={0}, use_global_device_ids=true | all-gather | bytes 36864 | tf_op jit(solution)/shard_map/all_gather | solution.py:78
  110.0 6.2 %fusion.5 = f32[128,34]{1,0:T(8,128)S(1)} fusion(f32[128,8192]{1,0:T(8,128)} %copy-done.2, f32[8192]{0:T(1024)S(1)} %all_gather.38, f32[128]{0:T(128)S(1)} %multiply_subtract_fusion.3, f32[8192,32]{0,1:T(8,128)S(1)} %copy-done.3, f32[8192,1]{0,1:T(1,128)S(1)} %broadcast_in_dim.10, f32[8192,1]{0,1:T(1,128)S(1)} %bitcast.84), kind=kOutput, calls=%fused_computation.9 | convolution fusion | flops 431521792 | bytes 5359104 | tf_op jit(solution)/shard_map/dot_general | solution.py:80
  116.4 57.8 %psum.14 = f32[34,34]{1,0:T(8,128)S(1)} all-reduce(f32[34,34]{1,0:T(8,128)S(1)} %fusion.31), channel_id=1, replica_groups=mesh['pairs'=2,'src'=8,'tgt'=2] {'src','tgt'}, use_global_device_ids=true, to_apply=%region_8.9 | all-reduce | flops 1156 | bytes 9248 | tf_op jit(solution)/shard_map/psum | solution.py:82
  174.5 3.8 %fusion.12 = (f32[128]{0:T(128)S(1)}, f32[128,8192]{1,0:T(8,128)S(1)}) fusion(f32[8192]{0:T(1024)S(1)} %all_gather.38, f32[128,34]{1,0:T(8,128)S(1)} %fusion.28, f32[8192,32]{0,1:T(8,128)S(1)} %get-tuple-element.28, f32[8192,1]{0,1:T(1,128)S(1)} %bitcast.85, f32[8192,1]{0,1:T(1,128)S(1)} %broadcast_in_dim.10), kind=kOutput, calls=%fused_computation.20 | convolution fusion | flops 431521664 | bytes 5359104 | tf_op jit(solution)/shard_map/dot_general | solution.py:61
  184.1 3.3 %all-to-all-start.2 = ((f32[1,8,1024]{2,0,1:T(1,128)}), f32[1,8,1024]{2,0,1:T(1,128)S(1)}, u32[]{:S(2)}, u32[]{:S(2)}) async-start(f32[1,8,1024]{2,0,1:T(1,128)} %bitcast.16), calls=%async_computation.2 | async-start | bytes 65536 | tf_op jit(solution)/shard_map/all_to_all | solution.py:72
  187.4 3.7 %exponential_reduce_fusion = f32[8192]{0:T(1024)} fusion(f32[128,8192]{1,0:T(8,128)} %copy-done.1, f32[8192]{0:T(1024)} %fusion.13, f32[128]{0:T(128)S(1)} %multiply_subtract_fusion.2), kind=kLoop, calls=%fused_computation.5 | loop fusion | flops 4186112 | bytes 4260352 | tf_op jit(solution)/shard_map/reduce_sum | solution.py:70
  191.2 2.9 all-to-all-done.2
  194.1 3.3 %all-to-all-start.3 = ((f32[1,8,1024]{2,0,1:T(1,128)}), f32[1,8,1024]{2,0,1:T(1,128)S(1)}, u32[]{:S(2)}, u32[]{:S(2)}) async-start(f32[1,8,1024]{2,0,1:T(1,128)} %bitcast.17), calls=%async_computation.3 | async-start | bytes 65536 | tf_op jit(solution)/shard_map/all_to_all | solution.py:73
  197.4 6.6 %all-to-all-done.3 = f32[1,8,1024]{2,0,1:T(1,128)S(1)} async-done(((f32[1,8,1024]{2,0,1:T(1,128)}), f32[1,8,1024]{2,0,1:T(1,128)S(1)}, u32[]{:S(2)}, u32[]{:S(2)}) %all-to-all-start.3) | async-done | bytes 32800 | tf_op jit(solution)/shard_map/all_to_all | solution.py:73
  204.1 30.6 %all_gather.43 = f32[8192]{0:T(1024)S(1)} all-gather(f32[1024]{0:T(1024)S(1)} %multiply_subtract_fusion), channel_id=1, replica_groups=mesh['pairs'=2,'src'=8,'tgt'=2] {'src'}, dimensions={0}, use_global_device_ids=true | all-gather | bytes 36864 | tf_op jit(solution)/shard_map/all_gather | solution.py:78
  234.7 6.2 %fusion = f32[128,34]{1,0:T(8,128)S(1)} fusion(f32[128,8192]{1,0:T(8,128)} %copy-done.1, f32[8192]{0:T(1024)S(1)} %all_gather.43, f32[128]{0:T(128)S(1)} %multiply_subtract_fusion.2, f32[8192,32]{0,1:T(8,128)S(1)} %copy-done.3, f32[8192,1]{0,1:T(1,128)S(1)} %broadcast_in_dim.10, f32[8192,1]{0,1:T(1,128)S(1)} %bitcast.86), kind=kOutput, calls=%fused_computation | convolution fusion | flops 431521792 | bytes 5359104 | tf_op jit(solution)/shard_map/dot_general | solution.py:80
  241.1 57.6 %psum.15 = f32[34,34]{1,0:T(8,128)S(1)} all-reduce(f32[34,34]{1,0:T(8,128)S(1)} %fusion.30), channel_id=1, replica_groups=mesh['pairs'=2,'src'=8,'tgt'=2] {'src','tgt'}, use_global_device_ids=true, to_apply=%region_15.16 | all-reduce | flops 1156 | bytes 9248 | tf_op jit(solution)/shard_map/psum | solution.py:82
  (43 shorter events, 19.1 us)
Async XLA Ops:
  0.6 20.9 %copy-start = (f32[34,34]{1,0:T(8,128)S(1)}, f32[34,34]{1,0:T(8,128)}, u32[]{:S(2)}) copy-start(f32[34,34]{1,0:T(8,128)} %param.7) | copy-start | bytes 13876
  0.6 9.2 %collective-permute-start = (f32[8192,4]{0,1:T(4,128)}, f32[8192,4]{0,1:T(4,128)S(1)}, u32[]{:S(2)}, u32[]{:S(2)}) collective-permute-start(f32[8192,4]{0,1:T(4,128)} %param.5), channel_id=1, source_target_pairs={{0,14},{2,0},{4,2},{6,4},{8,6},{10,8},{12,10},{14,12},{1,15},{3,1}... | collective-permute-start | bytes 393224 | tf_op jit(solution)/shard_map/ppermute | solution.py:18
  10.8 7.2 %collective-permute-start.1 = (f32[8192,8]{0,1:T(8,128)S(1)}, f32[8192,8]{0,1:T(8,128)S(1)}, u32[]{:S(2)}, u32[]{:S(2)}) collective-permute-start(f32[8192,8]{0,1:T(8,128)S(1)} %pad_maximum_fusion.7), channel_id=1, source_target_pairs={{0,12},{2,14},{4,0},{6,2},{8,4},{10,6},{12,8},{14,10},{1,13},{3,15... | collective-permute-start | bytes 786440 | tf_op jit(solution)/shard_map/ppermute | solution.py:18
  19.0 24.2 %collective-permute-start.2 = (f32[8192,16]{0,1:T(8,128)S(1)}, f32[8192,16]{0,1:T(8,128)S(1)}, u32[]{:S(2)}, u32[]{:S(2)}) collective-permute-start(f32[8192,16]{0,1:T(8,128)S(1)} %pad_maximum_fusion.6), channel_id=1, source_target_pairs={{0,8},{2,10},{4,12},{6,14},{8,0},{10,2},{12,4},{14,6},{1,9},{3,11}... | collective-permute-start | bytes 1572872 | tf_op jit(solution)/shard_map/ppermute | solution.py:18
  21.8 24.9 %copy-start.4 = (f32[8192]{0:T(1024)S(1)}, f32[8192]{0:T(1024)}, u32[]{:S(2)}) copy-start(f32[8192]{0:T(1024)} %param.6) | copy-start | bytes 98308
  50.5 5.8 %copy-start.2 = (f32[128,8192]{1,0:T(8,128)}, f32[128,8192]{1,0:T(8,128)S(1)}, u32[]{:S(2)}) copy-start(f32[128,8192]{1,0:T(8,128)S(1)} %get-tuple-element.38) | copy-start | bytes 12582916
  55.2 54.8 %copy-start.3 = (f32[8192,32]{0,1:T(8,128)S(1)}, f32[8192,32]{0,1:T(8,128)}, u32[]{:S(2)}) copy-start(f32[8192,32]{0,1:T(8,128)} %get-tuple-element.27) | copy-start | bytes 3145732
  56.3 13.0 %all-to-all-start = ((f32[1,8,1024]{2,0,1:T(1,128)}), f32[1,8,1024]{2,0,1:T(1,128)S(1)}, u32[]{:S(2)}, u32[]{:S(2)}) async-start(f32[1,8,1024]{2,0,1:T(1,128)} %bitcast.8), calls=%async_computation | async-start | bytes 65536 | tf_op jit(solution)/shard_map/all_to_all | solution.py:72
  69.4 10.0 %all-to-all-start.1 = ((f32[1,8,1024]{2,0,1:T(1,128)}), f32[1,8,1024]{2,0,1:T(1,128)S(1)}, u32[]{:S(2)}, u32[]{:S(2)}) async-start(f32[1,8,1024]{2,0,1:T(1,128)} %bitcast.9), calls=%async_computation.1 | async-start | bytes 65536 | tf_op jit(solution)/shard_map/all_to_all | solution.py:73
  178.3 5.8 %copy-start.1 = (f32[128,8192]{1,0:T(8,128)}, f32[128,8192]{1,0:T(8,128)S(1)}, u32[]{:S(2)}) copy-start(f32[128,8192]{1,0:T(8,128)S(1)} %get-tuple-element.40) | copy-start | bytes 12582916
  182.9 51.8 %copy-start.5 = (f32[128]{0:T(128)}, f32[128]{0:T(128)S(1)}, u32[]{:S(2)}) copy-start(f32[128]{0:T(128)S(1)} %multiply_subtract_fusion.2) | copy-start | bytes 1540
  184.1 10.0 %all-to-all-start.2 = ((f32[1,8,1024]{2,0,1:T(1,128)}), f32[1,8,1024]{2,0,1:T(1,128)S(1)}, u32[]{:S(2)}, u32[]{:S(2)}) async-start(f32[1,8,1024]{2,0,1:T(1,128)} %bitcast.16), calls=%async_computation.2 | async-start | bytes 65536 | tf_op jit(solution)/shard_map/all_to_all | solution.py:72
  194.1 10.0 %all-to-all-start.3 = ((f32[1,8,1024]{2,0,1:T(1,128)}), f32[1,8,1024]{2,0,1:T(1,128)S(1)}, u32[]{:S(2)}, u32[]{:S(2)}) async-start(f32[1,8,1024]{2,0,1:T(1,128)} %bitcast.17), calls=%async_computation.3 | async-start | bytes 65536 | tf_op jit(solution)/shard_map/all_to_all | solution.py:73
